TPU v7x, 32 devices: a whole 2x2x4 slice. The times are simulated.
32 devices in a mesh: groups: 2 (over y), wide: 4 (over z), narrow: 2 (over x), inner: 2 (over core).
Axes of the slice: x: 2, y: 2, z: 4, core: 2. Of those that a mesh axis runs over, the one named last changes fastest.
Arguments:
- tokens: bfloat16 [128, 6144], P(('groups', 'wide'), ('narrow', 'inner')), parts along dimension 0, may hold values from -6 to 6
- cotangent: bfloat16 [128, 6144], P(('groups', 'wide'), ('narrow', 'inner')), parts along dimension 0, may hold values from -3 to 3
- w_gate: bfloat16 [6144, 16384], P(('narrow', 'inner'), 'wide'), may hold values from -0.078125 to 0.078125
- w_up: bfloat16 [6144, 16384], P(('narrow', 'inner'), 'wide'), may hold values from -0.078125 to 0.078125
- w_down: bfloat16 [16384, 6144], P('wide', ('narrow', 'inner')), may hold values from -0.046875 to 0.046875
Outputs:
- output: bfloat16 [128, 6144], P(('groups', 'wide'), ('narrow', 'inner')), parts along dimension 0
- grad_input: bfloat16 [128, 6144], P(('groups', 'wide'), ('narrow', 'inner')), parts along dimension 0
- grad_wgate: bfloat16 [12288, 16384], P(('groups', 'narrow', 'inner'), 'wide'), parts along dimension 0
- grad_wup: bfloat16 [12288, 16384], P(('groups', 'narrow', 'inner'), 'wide'), parts along dimension 0
- grad_wdown: bfloat16 [32768, 6144], P(('groups', 'wide'), ('narrow', 'inner')), parts along dimension 0
There are 2 independent parts, one for each index of `groups`. A program takes and returns all parts, laid end to end along the dimension named above; an argument that names none is the same for every part. Nothing has to cross between parts.
All inputs are finite; a program needn't handle non-finite values.
Results may differ from a plain program's by a relative error of at most 0.012.
Values may be sent and summed in bfloat16 or wider, within the bound.
No kernel may reach another device: no remote copies, remote signals or barrier semaphores. Data moves between devices by JAX's collectives and lax.ppermute only.
A program may use at most 192 MiB of HBM per device.

v0:
```python
import jax
import jax.numpy as jnp
from jax import lax
from jax.sharding import PartitionSpec as P


def contract_last(left, right):
    return lax.dot_general(
        left, right, (((1,), (1,)), ((), ())), preferred_element_type=jnp.float32
    )


def contract_first(left, right):
    return lax.dot_general(
        left, right, (((0,), (0,)), ((), ())), preferred_element_type=jnp.float32
    )


def activate(gate, up):
    return (gate * jax.nn.sigmoid(gate) * up).astype(jnp.bfloat16)


def grad_parts(gate, up, upstream):
    sigmoid_gate = jax.nn.sigmoid(gate)
    grad_gate = (upstream * up * sigmoid_gate * (1.0 + gate * (1.0 - sigmoid_gate))).astype(
        jnp.bfloat16
    )
    grad_up = (upstream * gate * sigmoid_gate).astype(jnp.bfloat16)
    return (grad_gate, grad_up)


def body(tokens, cotangent, w_gate, w_up, w_down):
    gathered = lax.all_gather(tokens, "wide", axis=0, tiled=True)
    gate_part = jnp.dot(gathered, w_gate, preferred_element_type=jnp.float32)
    up_part = jnp.dot(gathered, w_up, preferred_element_type=jnp.float32)
    gate, up = lax.psum((gate_part, up_part), ("narrow", "inner"))
    hidden = activate(gate, up)
    output = lax.psum_scatter(
        jnp.dot(hidden, w_down, preferred_element_type=jnp.float32).astype(jnp.bfloat16),
        "wide",
        scatter_dimension=0,
        tiled=True,
    )
    cot_all = lax.all_gather(cotangent, "wide", axis=0, tiled=True)
    upstream_part = contract_last(cot_all, w_down)
    grad_wdown = contract_first(hidden, cot_all).astype(jnp.bfloat16)
    upstream = lax.psum(upstream_part, ("narrow", "inner"))
    grad_gate, grad_up = grad_parts(gate, up, upstream)
    grad_input = lax.psum_scatter(
        (contract_last(grad_gate, w_gate) + contract_last(grad_up, w_up)).astype(jnp.bfloat16),
        "wide",
        scatter_dimension=0,
        tiled=True,
    )
    grad_wgate = contract_first(gathered, grad_gate).astype(jnp.bfloat16)
    grad_wup = contract_first(gathered, grad_up).astype(jnp.bfloat16)
    return (output, grad_input, grad_wgate, grad_wup, grad_wdown)


def solution(mesh):
    return jax.shard_map(
        body,
        mesh=mesh,
        in_specs=(
            P(("groups", "wide"), ("narrow", "inner")),
            P(("groups", "wide"), ("narrow", "inner")),
            P(("narrow", "inner"), "wide"),
            P(("narrow", "inner"), "wide"),
            P("wide", ("narrow", "inner")),
        ),
        out_specs=(
            P(("groups", "wide"), ("narrow", "inner")),
            P(("groups", "wide"), ("narrow", "inner")),
            P(("groups", "narrow", "inner"), "wide"),
            P(("groups", "narrow", "inner"), "wide"),
            P(("groups", "wide"), ("narrow", "inner")),
        ),
        check_vma=False,
    )
```

profile of v0, /device:TPU:0, one launch (start us, length us, event | category | flops | bytes accessed | tf_op | source)
XLA Modules:
  0.0 206.2 jit_solution(17270711638761119251)
XLA Ops:
  7.2 0.0 all-reduce.3.cloned.1.call-start
  7.2 0.0 copy-start
  7.2 15.8 %all_gather.6 = bf16[64,1536]{1,0:T(8,128)(2,1)S(1)} all-gather(bf16[16,1536]{1,0:T(8,128)(2,1)} %param.5), channel_id=1, replica_groups=mesh['groups'=2,'wide'=4,'narrow'=2,'inner'=2] {'wide'}, dimensions={0}, use_global_device_ids=true | all-gather | bytes 245760 | tf_op jit(solution)/shard_map/all_gather | solution.py:33
  23.0 0.0 slice-start
  23.0 0.0 slice-start.1
  23.0 8.0 %fusion.4 = f32[64,4096]{1,0:T(8,128)} fusion(bf16[64,1536]{1,0:T(8,128)(2,1)S(1)} %all_gather.6, bf16[1536,4096]{1,0:T(8,128)(2,1)} %param.8), kind=kOutput, calls=%fused_computation.13 | convolution fusion | flops 805306368 | bytes 13828096 | tf_op jit(solution)/shard_map/dot_general | solution.py:35
  31.0 0.0 copy-done
  31.0 0.0 copy-start.1
  31.0 0.0 slice-start.2
  31.0 3.3 %fusion.3 = f32[64,4096]{1,0:T(8,128)} fusion(bf16[64,1536]{1,0:T(8,128)(2,1)S(1)} %all_gather.6, bf16[1536,4096]{1,0:T(8,128)(2,1)S(1)} %copy-done), kind=kOutput, calls=%fused_computation.12 | convolution fusion | flops 805306368 | bytes 13828096 | tf_op jit(solution)/shard_map/dot_general | solution.py:34
  34.3 0.0 copy-done.1
  34.3 14.0 %all_gather.7 = bf16[64,1536]{1,0:T(8,128)(2,1)S(1)} all-gather(bf16[16,1536]{1,0:T(8,128)(2,1)S(1)} %copy-done.1), channel_id=1, replica_groups=mesh['groups'=2,'wide'=4,'narrow'=2,'inner'=2] {'wide'}, dimensions={0}, use_global_device_ids=true | all-gather | bytes 245760 | tf_op jit(solution)/shard_map/all_gather | solution.py:44
  48.3 0.0 slice-done
  48.3 0.0 slice-done.1
  48.3 0.0 slice-done.2
  48.3 4.9 %fusion.5 = f32[64,4096]{1,0:T(8,128)} fusion(bf16[64,1536]{1,0:T(8,128)(2,1)S(1)} %all_gather.7, bf16[4096,1536]{1,0:T(8,128)(2,1)S(1)} %bitcast.23), kind=kOutput, calls=%fused_computation.14 | convolution fusion | flops 805306368 | bytes 13828096 | tf_op jit(solution)/shard_map/dot_general | solution.py:8
  53.2 0.0 all-reduce.3.cloned.1.call-update
  53.2 0.0 reduce-scatter.3.cloned.1.call-start
  53.3 69.9 %all-reduce.3.cloned.1.call-done = (f32[64,4096]{1,0:T(8,128)}, f32[64,4096]{1,0:T(8,128)}, f32[64,4096]{1,0:T(8,128)}) async-done(((f32[64,4096]{1,0:T(8,128)}, f32[64,4096]{1,0:T(8,128)}, f32[64,4096]{1,0:T(8,128)}), (f32[64,4096]{1,0:T(8,128)}, f32[64,4096]{1,0:T(8,128)}, f32[64,4096]{1,0:T(8,128)})) %all-reduce.3.cloned.1.call-update) | async-done | bytes 3145744 | tf_op jit(solution)/shard_map/psum | solution.py:36
  123.2 2.4 %multiply_convert_fusion = (bf16[64,4096]{1,0:T(8,128)(2,1)S(1)}, bf16[64,4096]{1,0:T(8,128)(2,1)S(1)}, bf16[64,4096]{1,0:T(8,128)(2,1)S(1)}) fusion(f32[64,4096]{1,0:T(8,128)} %get-tuple-element.12, f32[64,4096]{1,0:T(8,128)} %get-tuple-element.11, f32[64,4096]{1,0:T(8,128)} %get-tuple-element.10), kind=kLoop, calls=%fused_computation.8 | loop fusion | flops 4194304 | bytes 4718592 | tf_op jit(solution)/shard_map/convert_element_type | solution.py:28
  125.6 0.0 slice-start.3
  125.6 0.0 slice-start.4
  125.6 8.7 %fusion.6 = f32[64,1536]{1,0:T(8,128)S(1)} fusion(bf16[64,4096]{1,0:T(8,128)(2,1)S(1)} %get-tuple-element.14, bf16[1536,4096]{1,0:T(8,128)(2,1)} %param.7), kind=kOutput, calls=%fused_computation.15 | convolution fusion | flops 805306368 | bytes 13500416 | tf_op jit(solution)/shard_map/dot_general | solution.py:8
  134.3 0.0 slice-start.5
  134.3 6.6 %fusion = bf16[1536,4096]{0,1:T(8,128)(2,1)} fusion(bf16[64,4096]{1,0:T(8,128)(2,1)S(1)} %get-tuple-element.14, bf16[64,1536]{1,0:T(8,128)(2,1)S(1)} %all_gather.6), kind=kOutput, calls=%fused_computation.3 | convolution fusion | flops 811597824 | bytes 13303808 | tf_op jit(solution)/shard_map/dot_general | solution.py:14
  140.9 0.0 slice-done.3
  140.9 0.0 slice-done.4
  140.9 0.0 slice-done.5
  141.0 3.0 %convolution_convert_fusion.3 = bf16[64,1536]{1,0:T(8,128)(2,1)} fusion(bf16[64,4096]{1,0:T(8,128)(2,1)S(1)} %get-tuple-element.15, bf16[4096,1536]{1,0:T(8,128)(2,1)S(1)} %bitcast.25), kind=kOutput, calls=%fused_computation.7 | convolution fusion | flops 805404672 | bytes 13303808 | tf_op jit(solution)/shard_map/dot_general | solution.py:39
  143.9 0.0 reduce-scatter.3.cloned.1.call-update
  144.0 0.2 reduce-scatter.5.cloned.1.call-start
  144.2 6.4 %fusion.1 = bf16[1536,4096]{0,1:T(8,128)(2,1)} fusion(bf16[64,4096]{1,0:T(8,128)(2,1)S(1)} %get-tuple-element.13, bf16[64,1536]{1,0:T(8,128)(2,1)S(1)} %all_gather.6), kind=kOutput, calls=%fused_computation.4 | convolution fusion | flops 811597824 | bytes 13303808 | tf_op jit(solution)/shard_map/dot_general | solution.py:14
  150.6 9.2 %fusion.2 = bf16[64,1536]{1,0:T(8,128)(2,1)} fusion(f32[64,1536]{1,0:T(8,128)S(1)} %fusion.6, bf16[64,4096]{1,0:T(8,128)(2,1)S(1)} %get-tuple-element.13, bf16[1536,4096]{1,0:T(8,128)(2,1)} %param.8), kind=kOutput, calls=%fused_computation.6 | convolution fusion | flops 805502976 | bytes 13697024 | tf_op jit(solution)/shard_map/dot_general | solution.py:8
  159.8 0.0 reduce-scatter.5.cloned.1.call-update
  159.8 6.6 %convolution_convert_fusion = bf16[4096,1536]{1,0:T(8,128)(2,1)} fusion(bf16[64,4096]{1,0:T(8,128)(2,1)S(1)} %get-tuple-element.15, bf16[64,1536]{1,0:T(8,128)(2,1)S(1)} %all_gather.7), kind=kOutput, calls=%fused_computation | convolution fusion | flops 811597824 | bytes 13303808 | tf_op jit(solution)/shard_map/dot_general | solution.py:14
  166.4 16.6 %copy.10 = bf16[1536,4096]{1,0:T(8,128)(2,1)} copy(bf16[1536,4096]{0,1:T(8,128)(2,1)} %fusion) | data formatting | bytes 25165824
  183.0 16.6 %copy.11 = bf16[1536,4096]{1,0:T(8,128)(2,1)} copy(bf16[1536,4096]{0,1:T(8,128)(2,1)} %fusion.1) | data formatting | bytes 25165824
  199.6 0.0 reduce-scatter.3.cloned.1.call-done
  199.6 0.0 reduce-scatter.5.cloned.1.call-done
  (2 shorter events, 0.0 us)
Async XLA Ops:
  7.2 116.0 %all-reduce.3.cloned.1.call-start = ((), (), s32[]{:S(2)}) async-start(), calls=%async_computation.4 | async-start | bytes 6291456 | tf_op jit(solution)/shard_map/psum | solution.py:36
  7.2 23.8 %copy-start = (bf16[1536,4096]{1,0:T(8,128)(2,1)S(1)}, bf16[1536,4096]{1,0:T(8,128)(2,1)}, u32[]{:S(2)}) copy-start(bf16[1536,4096]{1,0:T(8,128)(2,1)} %param.7) | copy-start | bytes 37748740
  23.0 25.3 %slice-start = ((s8[12582912]{0:T(1024)(128)(4,1)}), s8[4194304]{0:T(1024)(128)(4,1)S(1)}, s32[]{:S(2)}) async-start(s8[12582912]{0:T(1024)(128)(4,1)} %bitcast.22), calls=%async_computation.5 | async-start | bytes 8388608
  23.0 25.3 %slice-start.1 = ((s8[12582912]{0:T(1024)(128)(4,1)}), s8[4194304]{0:T(1024)(128)(4,1)S(1)}, s32[]{:S(2)}) async-start(s8[12582912]{0:T(1024)(128)(4,1)} %bitcast.22), calls=%async_computation.6 | async-start | bytes 8388608
  31.0 3.3 %copy-start.1 = (bf16[16,1536]{1,0:T(8,128)(2,1)S(1)}, bf16[16,1536]{1,0:T(8,128)(2,1)}, u32[]{:S(2)}) copy-start(bf16[16,1536]{1,0:T(8,128)(2,1)} %param.6) | copy-start | bytes 147460
  31.0 17.3 %slice-start.2 = ((s8[12582912]{0:T(1024)(128)(4,1)}), s8[4194304]{0:T(1024)(128)(4,1)S(1)}, s32[]{:S(2)}) async-start(s8[12582912]{0:T(1024)(128)(4,1)} %bitcast.22), calls=%async_computation.7 | async-start | bytes 8388608
  53.2 146.4 %reduce-scatter.3.cloned.1.call-start = ((), (), s32[]{:S(2)}) async-start(), calls=%async_computation.2 | async-start | bytes 245760 | tf_op jit(solution)/shard_map/reduce_scatter | solution.py:38
  125.6 15.3 %slice-start.3 = ((s8[12582912]{0:T(1024)(128)(4,1)}), s8[4194304]{0:T(1024)(128)(4,1)S(1)}, s32[]{:S(2)}) async-start(s8[12582912]{0:T(1024)(128)(4,1)} %bitcast.24), calls=%async_computation.8 | async-start | bytes 8388608
  125.6 15.3 %slice-start.4 = ((s8[12582912]{0:T(1024)(128)(4,1)}), s8[4194304]{0:T(1024)(128)(4,1)S(1)}, s32[]{:S(2)}) async-start(s8[12582912]{0:T(1024)(128)(4,1)} %bitcast.24), calls=%async_computation.9 | async-start | bytes 8388608
  134.3 6.6 %slice-start.5 = ((s8[12582912]{0:T(1024)(128)(4,1)}), s8[4194304]{0:T(1024)(128)(4,1)S(1)}, s32[]{:S(2)}) async-start(s8[12582912]{0:T(1024)(128)(4,1)} %bitcast.24), calls=%async_computation.10 | async-start | bytes 8388608
  144.0 55.7 %reduce-scatter.5.cloned.1.call-start = ((), (), s32[]{:S(2)}) async-start(), calls=%async_computation.3 | async-start | bytes 245760 | tf_op jit(solution)/shard_map/reduce_scatter | solution.py:49
Sparse Core Ops, SparseCore 0:
  53.3 69.8 all-reduce.2
  144.1 19.4 reduce-scatter.2
  166.5 17.5 reduce-scatter.4
where the time goes:
time: 207 us; the launch traced here: 206 us
  waiting for transfers between devices  70 us (34%)
  matrix products  56.6 us (27%)
  local copies, waits for them, and re-layouts  33.3 us (16%)
  blocking collectives  29.8 us (14%)
  between operations  13.8 us (7%)
  other arithmetic  2.4 us (1%)
    psum x1, waiting for transfers between devices, body(): gate, up = lax.psum((gate_part, up_part), ('narrow', 'inner'))  69.9 us
    unnamed x18, local copies, waits for them, and re-layouts  33.3 us
    dot_general x3, matrix products, contract_last(): lax.dot_general(left, right, (((1,), (1,)), ((), ())), preferred_element_...  22.7 us
    dot_general x3, matrix products, contract_first(): lax.dot_general(left, right, (((0,), (0,)), ((), ())), preferred_element_...  19.7 us
    all_gather x1, blocking collectives, body(): gathered = lax.all_gather(tokens, 'wide', axis=0, tiled=True)  15.8 us
    all_gather x1, blocking collectives, body(): cot_all = lax.all_gather(cotangent, 'wide', axis=0, tiled=True)  14 us
    dot_general x1, matrix products, body(): up_part = jnp.dot(gathered, w_up, preferred_element_type=jnp.float32)  7.99 us
  transfers between devices with their start and end apart: 3, of which 1 were waited for; matrix products, arithmetic and copies ran while one was open for 27% of the time, Pallas kernels for 0%

commit v1 on v0

--- a/solution.py
+++ b/solution.py
@@ -2,6 +2,10 @@
 import jax.numpy as jnp
 from jax import lax
 from jax.sharding import PartitionSpec as P
+
+
+def samples_finish(s0):
+    return jax.lax.psum(jax.lax.psum(s0, "inner"), "narrow")
 
 
 def contract_last(left, right):
@@ -33,7 +37,7 @@
     gathered = lax.all_gather(tokens, "wide", axis=0, tiled=True)
     gate_part = jnp.dot(gathered, w_gate, preferred_element_type=jnp.float32)
     up_part = jnp.dot(gathered, w_up, preferred_element_type=jnp.float32)
-    gate, up = lax.psum((gate_part, up_part), ("narrow", "inner"))
+    gate, up = samples_finish((gate_part, up_part))
     hidden = activate(gate, up)
     output = lax.psum_scatter(
         jnp.dot(hidden, w_down, preferred_element_type=jnp.float32).astype(jnp.bfloat16),

time: 207 us -> 247 us (1.19)
  waiting for transfers between devices: 70 us -> 105 us
  matrix products: 56.6 us -> 61.2 us
    psum x1 -> x3, waiting for transfers between devices: 69.9 us -> 104 us  [the longest x2 65.9 us: samples_finish(): return jax.lax.psum(jax.lax.psum(s0, 'inner'), 'narrow')]
    dot_general x3, matrix products: 22.7 us -> 27.5 us  [contract_last(): lax.dot_general(left, right, (((1,), (1,)), ((), ())), preferred_element_...]
    unnamed x18 -> x12, local copies, waits for them, and re-layouts: 33.3 us -> 33.2 us
  transfers between devices with their start and end apart: 3 -> 5, of which waited for: 1 -> 2; matrix products, arithmetic and copies ran while one was open for 27% -> 26% of each run, Pallas kernels for 0% -> 0%
where the time goes in v1:
time: 247 us; the launch traced here: 246 us
  waiting for transfers between devices  105 us (43%)
  matrix products  61.2 us (25%)
  local copies, waits for them, and re-layouts  33.2 us (13%)
  blocking collectives  29.8 us (12%)
  between operations  13.8 us (6%)
    psum x2, waiting for transfers between devices, samples_finish(): return jax.lax.psum(jax.lax.psum(s0, 'inner'), 'narrow')  65.9 us
    psum x1, waiting for transfers between devices, body(): upstream = lax.psum(upstream_part, ('narrow', 'inner'))  38.3 us
    unnamed x12, local copies, waits for them, and re-layouts  33.2 us
    dot_general x3, matrix products, contract_last(): lax.dot_general(left, right, (((1,), (1,)), ((), ())), preferred_element_...  27.5 us
    dot_general x3, matrix products, contract_first(): lax.dot_general(left, right, (((0,), (0,)), ((), ())), preferred_element_...  19.7 us
    all_gather x1, blocking collectives, body(): gathered = lax.all_gather(tokens, 'wide', axis=0, tiled=True)  15.8 us
    all_gather x1, blocking collectives, body(): cot_all = lax.all_gather(cotangent, 'wide', axis=0, tiled=True)  14 us
    dot_general x1, matrix products, body(): up_part = jnp.dot(gathered, w_up, preferred_element_type=jnp.float32)  7.84 us
  transfers between devices with their start and end apart: 5, of which 2 were waited for; matrix products, arithmetic and copies ran while one was open for 26% of the time, Pallas kernels for 0%

profile of v1, /device:TPU:0, one launch (start us, length us, event | category | flops | bytes accessed | tf_op | source)
XLA Modules:
  0.0 246.1 jit_solution(4538748165556928217)
XLA Ops:
  7.2 0.0 all-reduce.8.cloned.1.call-start
  7.2 0.0 copy-start
  7.2 15.8 %all_gather.6 = bf16[64,1536]{1,0:T(8,128)(2,1)S(1)} all-gather(bf16[16,1536]{1,0:T(8,128)(2,1)} %param.5), channel_id=1, replica_groups=mesh['groups'=2,'wide'=4,'narrow'=2,'inner'=2] {'wide'}, dimensions={0}, use_global_device_ids=true | all-gather | bytes 245760 | tf_op jit(solution)/shard_map/all_gather | solution.py:37
  23.0 7.8 %fusion.4 = f32[64,4096]{1,0:T(8,128)} fusion(bf16[64,1536]{1,0:T(8,128)(2,1)S(1)} %all_gather.6, bf16[1536,4096]{1,0:T(8,128)(2,1)} %param.8), kind=kOutput, calls=%fused_computation.13 | convolution fusion | flops 805306368 | bytes 13828096 | tf_op jit(solution)/shard_map/dot_general | solution.py:39
  30.9 0.0 copy-done
  30.9 0.0 copy-start.1
  30.9 3.3 %fusion.3 = f32[64,4096]{1,0:T(8,128)} fusion(bf16[64,1536]{1,0:T(8,128)(2,1)S(1)} %all_gather.6, bf16[1536,4096]{1,0:T(8,128)(2,1)S(1)} %copy-done), kind=kOutput, calls=%fused_computation.12 | convolution fusion | flops 805306368 | bytes 13828096 | tf_op jit(solution)/shard_map/dot_general | solution.py:38
  34.1 0.0 all-reduce.8.cloned.1.call-update
  34.2 0.0 all-reduce.6.cloned.1.call-start
  34.2 0.0 copy-done.1
  34.2 14.0 %all_gather.7 = bf16[64,1536]{1,0:T(8,128)(2,1)S(1)} all-gather(bf16[16,1536]{1,0:T(8,128)(2,1)S(1)} %copy-done.1), channel_id=1, replica_groups=mesh['groups'=2,'wide'=4,'narrow'=2,'inner'=2] {'wide'}, dimensions={0}, use_global_device_ids=true | all-gather | bytes 245760 | tf_op jit(solution)/shard_map/all_gather | solution.py:48
  48.3 9.6 %fusion.5 = f32[64,4096]{1,0:T(8,128)} fusion(bf16[64,1536]{1,0:T(8,128)(2,1)S(1)} %all_gather.7, bf16[4096,1536]{1,0:T(8,128)(2,1)} %param.9), kind=kOutput, calls=%fused_computation.14 | convolution fusion | flops 805306368 | bytes 13828096 | tf_op jit(solution)/shard_map/dot_general | solution.py:12
  57.9 0.0 all-reduce.6.cloned.1.call-update
  57.9 0.0 all-reduce.10.cloned.1.call-start
  58.0 0.0 all-reduce.8.cloned.1.call-done
  58.0 0.7 all-reduce.10.cloned.1.call-update
  58.7 0.2 reduce-scatter.3.cloned.1.call-start
  58.9 38.3 %all-reduce.6.cloned.1.call-done = f32[64,4096]{1,0:T(8,128)} async-done(((f32[64,4096]{1,0:T(8,128)}), f32[64,4096]{1,0:T(8,128)}) %all-reduce.6.cloned.1.call-update) | async-done | bytes 1048592 | tf_op jit(solution)/shard_map/psum | solution.py:51
  97.2 65.9 %all-reduce.10.cloned.1.call-done = (f32[64,4096]{1,0:T(8,128)}, f32[64,4096]{1,0:T(8,128)}) async-done(((f32[64,4096]{1,0:T(8,128)}, f32[64,4096]{1,0:T(8,128)}), (f32[64,4096]{1,0:T(8,128)}, f32[64,4096]{1,0:T(8,128)})) %all-reduce.10.cloned.1.call-update) | async-done | bytes 2097168 | tf_op jit(solution)/shard_map/psum | solution.py:8
  163.1 2.4 multiply_convert_fusion
  165.5 0.0 slice-start
  165.5 0.0 slice-start.1
  165.5 8.7 %fusion.6 = f32[64,1536]{1,0:T(8,128)S(1)} fusion(bf16[64,4096]{1,0:T(8,128)(2,1)S(1)} %get-tuple-element.15, bf16[1536,4096]{1,0:T(8,128)(2,1)} %param.7), kind=kOutput, calls=%fused_computation.15 | convolution fusion | flops 805306368 | bytes 13500416 | tf_op jit(solution)/shard_map/dot_general | solution.py:12
  174.2 0.0 slice-start.2
  174.2 6.6 %fusion = bf16[1536,4096]{0,1:T(8,128)(2,1)} fusion(bf16[64,4096]{1,0:T(8,128)(2,1)S(1)} %get-tuple-element.15, bf16[64,1536]{1,0:T(8,128)(2,1)S(1)} %all_gather.6), kind=kOutput, calls=%fused_computation.3 | convolution fusion | flops 811597824 | bytes 13303808 | tf_op jit(solution)/shard_map/dot_general | solution.py:18
  180.8 0.0 slice-done
  180.8 0.0 slice-done.1
  180.8 0.0 slice-done.2
  180.8 3.0 %convolution_convert_fusion.3 = bf16[64,1536]{1,0:T(8,128)(2,1)} fusion(bf16[64,4096]{1,0:T(8,128)(2,1)S(1)} %get-tuple-element.16, bf16[4096,1536]{1,0:T(8,128)(2,1)S(1)} %bitcast.23), kind=kOutput, calls=%fused_computation.7 | convolution fusion | flops 805404672 | bytes 13303808 | tf_op jit(solution)/shard_map/dot_general | solution.py:43
  183.8 0.0 reduce-scatter.3.cloned.1.call-update
  183.8 0.3 reduce-scatter.5.cloned.1.call-start
  184.1 6.4 %fusion.1 = bf16[1536,4096]{0,1:T(8,128)(2,1)} fusion(bf16[64,4096]{1,0:T(8,128)(2,1)S(1)} %get-tuple-element.14, bf16[64,1536]{1,0:T(8,128)(2,1)S(1)} %all_gather.6), kind=kOutput, calls=%fused_computation.4 | convolution fusion | flops 811597824 | bytes 13303808 | tf_op jit(solution)/shard_map/dot_general | solution.py:18
  190.5 9.2 %fusion.2 = bf16[64,1536]{1,0:T(8,128)(2,1)} fusion(f32[64,1536]{1,0:T(8,128)S(1)} %fusion.6, bf16[64,4096]{1,0:T(8,128)(2,1)S(1)} %get-tuple-element.14, bf16[1536,4096]{1,0:T(8,128)(2,1)} %param.8), kind=kOutput, calls=%fused_computation.6 | convolution fusion | flops 805502976 | bytes 13697024 | tf_op jit(solution)/shard_map/dot_general | solution.py:12
  199.7 0.0 reduce-scatter.5.cloned.1.call-update
  199.7 6.6 %convolution_convert_fusion = bf16[4096,1536]{1,0:T(8,128)(2,1)} fusion(bf16[64,4096]{1,0:T(8,128)(2,1)S(1)} %get-tuple-element.16, bf16[64,1536]{1,0:T(8,128)(2,1)S(1)} %all_gather.7), kind=kOutput, calls=%fused_computation | convolution fusion | flops 811597824 | bytes 13303808 | tf_op jit(solution)/shard_map/dot_general | solution.py:18
  206.3 16.6 %copy.10 = bf16[1536,4096]{1,0:T(8,128)(2,1)} copy(bf16[1536,4096]{0,1:T(8,128)(2,1)} %fusion) | data formatting | bytes 25165824
  222.9 16.6 %copy.11 = bf16[1536,4096]{1,0:T(8,128)(2,1)} copy(bf16[1536,4096]{0,1:T(8,128)(2,1)} %fusion.1) | data formatting | bytes 25165824
  239.5 0.0 reduce-scatter.3.cloned.1.call-done
  239.5 0.0 reduce-scatter.5.cloned.1.call-done
  (1 shorter events, 0.0 us)
Async XLA Ops:
  7.2 50.8 %all-reduce.8.cloned.1.call-start = ((), (), s32[]{:S(2)}) async-start(), calls=%async_computation.5 | async-start | bytes 4194304 | tf_op jit(solution)/shard_map/psum | solution.py:8
  7.2 23.7 %copy-start = (bf16[1536,4096]{1,0:T(8,128)(2,1)S(1)}, bf16[1536,4096]{1,0:T(8,128)(2,1)}, u32[]{:S(2)}) copy-start(bf16[1536,4096]{1,0:T(8,128)(2,1)} %param.7) | copy-start | bytes 37748740
  30.9 3.3 %copy-start.1 = (bf16[16,1536]{1,0:T(8,128)(2,1)S(1)}, bf16[16,1536]{1,0:T(8,128)(2,1)}, u32[]{:S(2)}) copy-start(bf16[16,1536]{1,0:T(8,128)(2,1)} %param.6) | copy-start | bytes 147460
  34.2 63.1 %all-reduce.6.cloned.1.call-start = ((), (), s32[]{:S(2)}) async-start(), calls=%async_computation.3 | async-start | bytes 2097152 | tf_op jit(solution)/shard_map/psum | solution.py:51
  57.9 105.2 %all-reduce.10.cloned.1.call-start = ((), (), s32[]{:S(2)}) async-start(), calls=%async_computation.6 | async-start | bytes 4194304 | tf_op jit(solution)/shard_map/psum | solution.py:8
  58.7 180.9 %reduce-scatter.3.cloned.1.call-start = ((), (), s32[]{:S(2)}) async-start(), calls=%async_computation.2 | async-start | bytes 245760 | tf_op jit(solution)/shard_map/reduce_scatter | solution.py:42
  165.5 15.3 %slice-start = ((s8[12582912]{0:T(1024)(128)(4,1)}), s8[4194304]{0:T(1024)(128)(4,1)S(1)}, s32[]{:S(2)}) async-start(s8[12582912]{0:T(1024)(128)(4,1)} %bitcast.22), calls=%async_computation.7 | async-start | bytes 8388608
  165.5 15.3 %slice-start.1 = ((s8[12582912]{0:T(1024)(128)(4,1)}), s8[4194304]{0:T(1024)(128)(4,1)S(1)}, s32[]{:S(2)}) async-start(s8[12582912]{0:T(1024)(128)(4,1)} %bitcast.22), calls=%async_computation.8 | async-start | bytes 8388608
  174.2 6.6 %slice-start.2 = ((s8[12582912]{0:T(1024)(128)(4,1)}), s8[4194304]{0:T(1024)(128)(4,1)S(1)}, s32[]{:S(2)}) async-start(s8[12582912]{0:T(1024)(128)(4,1)} %bitcast.22), calls=%async_computation.9 | async-start | bytes 8388608
  183.8 55.7 %reduce-scatter.5.cloned.1.call-start = ((), (), s32[]{:S(2)}) async-start(), calls=%async_computation.4 | async-start | bytes 245760 | tf_op jit(solution)/shard_map/reduce_scatter | solution.py:53
Sparse Core Ops, SparseCore 0:
  34.3 22.6 all-reduce.7
  60.0 37.1 all-reduce.5
  99.6 63.4 all-reduce.9
  183.9 19.3 reduce-scatter.2
  206.0 17.5 reduce-scatter.4
